TPU v7x, 32 devices: a whole 2x2x4 slice. The times are simulated.
32 devices in a mesh: dp: 8 (over y, x, core), group: 4 (over z).
Axes of the slice: x: 2, y: 2, z: 4, core: 2. Of those that a mesh axis runs over, the one named last changes fastest.
Arguments:
- tokens: bfloat16 [8192, 2048], P('dp', 'group'), may hold values from -6 to 6
- gate_w: bfloat16 [2048, 1024], P('dp', 'group'), may hold values from -0.125 to 0.125
- up_w: bfloat16 [2048, 1024], P('dp', 'group'), may hold values from -0.125 to 0.125
- block_rows: int32 [32, 128], P('dp'), may hold values from 0 to 1023, as said below
- block_count: int32 [8], P('dp'), may hold values from 1 to 4, as said below
- route_gate: float32 [32, 128], P('dp'), may hold values from 0.05 to 1
- grad_hidden: bfloat16 [4096, 1024], P('dp', 'group'), may hold values from -6 to 6
Outputs:
- hidden: bfloat16 [4096, 1024], P('dp', 'group')
- grad_tokens: bfloat16 [8192, 2048], P('dp', 'group')
- grad_gate_w: float32 [2048, 1024], P('dp', 'group')
- grad_up_w: float32 [2048, 1024], P('dp', 'group')
Inputs may be any that keep to these rules, and one draw needn't show every extreme that they name: `block_rows`: the rows of one index of dp name 512 distinct tokens of its own 1024. The live slots of an index of dp are its first block_count ones; some index has all 4 live in every draw.
All inputs are finite; a program needn't handle non-finite values.
Results may differ from a plain program's by a relative error of at most 0.0049.
Values may be sent and summed in bfloat16 or wider, within the bound.
A program may use at most 64 MiB of HBM per device.

v0:
```python
import functools

import jax
import jax.numpy as jnp
from jax import lax
from jax.experimental import pallas as pl
from jax.experimental.pallas import tpu as pltpu
from jax.sharding import PartitionSpec as P

F32 = jnp.float32
BF16 = jnp.bfloat16
CUTS = 1
AHEAD = 3
HOP = 1
DELAY = 1
BOTH = (((0,), (0,)), ((), ()))
BACK = (((1,), (1,)), ((), ()))


def scattered(bits, number):
    return sum(((number >> at) & 1) << bit for at, bit in enumerate(bits))


def kernel(
    n_dp,
    n_g,
    factor,
    tokens_in,
    gate_w,
    up_w,
    rows_in,
    count,
    route_in,
    grad_in,
    hidden,
    grad_tokens,
    grad_gate_w,
    grad_up_w,
    tokens,
    rows,
    route,
    grad_hidden,
    onehot,
    coef,
    routed,
    wg,
    wu,
    grads,
    part,
    outgoing,
    from_left,
    from_right,
    landed,
    sum_g,
    sum_u,
    stage_g,
    stage_u,
    got_g,
    got_u,
    own_sem,
    fwd_sem,
    ag_sem,
    w_send,
    w_recv,
    rs_send,
    left_sem,
    right_sem,
    h_send,
    h_recv,
    local_sem,
):
    n_blocks, block_len = rows.shape
    nb, blk = part.shape[0], part.shape[2]
    n_tok, fw = tokens.shape
    w_rows, width = gate_w.shape
    n_bits = n_dp.bit_length() - 1
    p = lax.axis_index("dp")
    z = lax.axis_index("group")

    def bit(k):
        return (p // 2**k) % 2

    def partner(k):
        return p + 2**k - bit(k) * 2 ** (k + 1)

    upper = list(range(1, n_bits))
    order_g = upper + [0]
    order_u = upper[::-1] + [0]

    copies_in = [
        pltpu.make_async_copy(source, dest, local_sem.at[i])
        for i, (source, dest) in enumerate(
            (
                (tokens_in, tokens),
                (rows_in, rows),
                (route_in, route),
                (gate_w, wg.at[pl.ds(p * w_rows, w_rows)]),
                (up_w, wu.at[pl.ds(p * w_rows, w_rows)]),
                (grad_in, grad_hidden),
            )
        )
    ]
    for copy in copies_in:
        copy.start()

    barrier = pltpu.get_barrier_semaphore()
    for k in range(n_bits):
        pl.semaphore_signal(barrier, inc=1, device_id={"dp": partner(k)})

    @pl.when(z > 0)
    def _():
        pl.semaphore_signal(barrier, inc=1, device_id={"group": z - 1})

    @pl.when(z < n_g - 1)
    def _():
        pl.semaphore_signal(barrier, inc=1, device_id={"group": z + 1})

    def pick(b):
        span = slice(b * block_len, (b + 1) * block_len)
        hot = lax.broadcasted_iota(jnp.int32, (n_tok, block_len), 0) == rows[b : b + 1, :]
        hot = jnp.where(hot, 1.0, 0.0).astype(BF16)
        onehot[:, span] = hot
        picked = lax.dot_general(hot, tokens[...], BOTH, preferred_element_type=F32)
        routed[z, span, :] = picked.astype(BF16)

    copies_in[0].wait()
    copies_in[1].wait()
    pick(0)
    sides = jnp.minimum(z, 1) + jnp.minimum(n_g - 1 - z, 1)
    pl.semaphore_wait(barrier, n_bits + sides)

    def weight_copies(which, phase):
        source, dest, order = ((gate_w, wg, order_g), (up_w, wu, order_u))[which]
        k = order[phase]
        done = order[:phase]
        base = p - sum(bit(j) * 2**j for j in done) if done else p
        copies = []
        for i in range(2**phase):
            c = base + scattered(done, i)
            place = dest.at[pl.ds(c * w_rows, w_rows)]
            copies.append(
                pltpu.make_async_remote_copy(
                    src_ref=source if phase == 0 else place,
                    dst_ref=dest.at[pl.ds(p * w_rows, w_rows)] if phase == 0 else place,
                    send_sem=w_send.at[which, phase],
                    recv_sem=w_recv.at[which, phase],
                    device_id={"dp": partner(k)},
                )
            )
        return copies

    def weight_start(phase):
        for which in range(2):
            for copy in weight_copies(which, phase):
                copy.start()

    def weight_wait(phase):
        for which in range(2):
            dest, order = ((wg, order_g), (wu, order_u))[which]
            span = dest.at[pl.ds(0, w_rows * 2**phase)]
            whole = pltpu.make_async_remote_copy(
                src_ref=span,
                dst_ref=span,
                send_sem=w_send.at[which, phase],
                recv_sem=w_recv.at[which, phase],
                device_id={"dp": partner(order[phase])},
            )
            whole.wait()

    def feature_copy(s, b, send_sem, to):
        place = routed.at[s, pl.ds(pl.multiple_of(b * blk, blk), blk)]
        return pltpu.make_async_remote_copy(
            src_ref=place,
            dst_ref=place,
            send_sem=send_sem,
            recv_sem=ag_sem.at[b, s],
            device_id={"group": to},
        )

    def own_left(b):
        return feature_copy(z, b, own_sem.at[b, 0], z - 1)

    def own_right(b):
        return feature_copy(z, b, own_sem.at[b, 1], z + 1)

    def own_start(b):
        @pl.when(z > 0)
        def _():
            own_left(b).start()

        @pl.when(z < n_g - 1)
        def _():
            own_right(b).start()

    def take(b, k):
        @pl.when(z - k >= 0)
        def _():
            feature_copy(z - k, b, fwd_sem.at[b, z - k], z).wait_recv()

            @pl.when(z < n_g - 1)
            def _():
                feature_copy(z - k, b, fwd_sem.at[b, z - k], z + 1).start()

        @pl.when(z + k < n_g)
        def _():
            feature_copy(z + k, b, fwd_sem.at[b, z + k], z).wait_recv()

            @pl.when(z > 0)
            def _():
                feature_copy(z + k, b, fwd_sem.at[b, z + k], z - 1).start()

    weight_start(0)
    cuts = block_len // blk
    for b in range(min(AHEAD, cuts)):
        own_start(b)
    for b in range(1, n_blocks):
        pick(b)
        for at in range(b * cuts, min(AHEAD, (b + 1) * cuts)):
            own_start(at)
    copies_in[2].wait()
    live = lax.broadcasted_iota(jnp.int32, (n_blocks, block_len), 0) < count[0]
    weights = jnp.where(live, route[...], 0.0)
    for b in range(n_blocks):
        turned = jnp.broadcast_to(weights[b : b + 1, :], (block_len, block_len)).T
        coef[b * block_len : (b + 1) * block_len, :] = turned
    for copy in copies_in[3:]:
        copy.wait()

    distance = 1
    for phase in range(n_bits):
        weight_wait(phase)
        if phase + 1 < n_bits:
            weight_start(phase + 1)
        if distance < n_g:
            take(0, distance)
            distance += 1
    for k in range(distance, n_g):
        take(0, k)

    def block_step(b):
        span = pl.ds(pl.multiple_of(b * blk, blk), blk)
        gate = jnp.zeros((blk, width), F32)
        up = jnp.zeros((blk, width), F32)
        for s in range(n_g):
            x = routed[s, span, :]
            gate += jnp.dot(x, wg[s * fw : (s + 1) * fw, :], preferred_element_type=F32)
            up += jnp.dot(x, wu[s * fw : (s + 1) * fw, :], preferred_element_type=F32)
        c = jnp.concatenate([coef[span, :]] * (width // coef.shape[1]), axis=1)
        sig = jax.nn.sigmoid(gate)
        act = gate * sig
        hidden[span, :] = (c * act * up).astype(BF16)
        scaled = grad_hidden[span, :].astype(F32) * c
        gg = (scaled * up * sig * (1.0 + gate * (1.0 - sig))).astype(BF16)
        gu = (scaled * act).astype(BF16)
        grads[span, :width] = gg
        grads[span, width:] = gu
        for d in range(n_g):
            back = lax.dot_general(
                gg, wg[d * fw : (d + 1) * fw, :], BACK, preferred_element_type=F32
            )
            back += lax.dot_general(
                gu, wu[d * fw : (d + 1) * fw, :], BACK, preferred_element_type=F32
            )
            part[b, d] = back

    def row_copy(b, d, right):
        return pltpu.make_async_remote_copy(
            src_ref=outgoing.at[b, d],
            dst_ref=(from_left if right else from_right).at[b, d],
            send_sem=rs_send.at[b, d],
            recv_sem=(left_sem if right else right_sem).at[b, d],
            device_id={"group": z + 1 if right else z - 1},
        )

    def flow_ends(b):
        @pl.when(z == 0)
        def _():
            for d in range(n_g - 1, 0, -1):
                outgoing[b, d] = part[b, d].astype(BF16)
                row_copy(b, d, True).start()

        @pl.when(z == n_g - 1)
        def _():
            for d in range(n_g - 1):
                outgoing[b, d] = part[b, d].astype(BF16)
                row_copy(b, d, False).start()

    def flow_inner(s):
        right_b = s - HOP * (z - 1)

        @pl.when((z > 0) & (z < n_g - 1) & (right_b >= 0) & (right_b < nb))
        def _():
            for k in range(n_g - 1, 0, -1):
                d = z + k

                @pl.when(d < n_g)
                def _():
                    row_copy(right_b, d, True).wait_recv()
                    outgoing[right_b, d] = (
                        part[right_b, d] + from_left[right_b, d].astype(F32)
                    ).astype(BF16)
                    row_copy(right_b, d, True).start()

        left_b = s - HOP * (n_g - 2 - z)

        @pl.when((z > 0) & (z < n_g - 1) & (left_b >= 0) & (left_b < nb))
        def _():
            for k in range(n_g - 1, 0, -1):
                d = z - k

                @pl.when(d >= 0)
                def _():
                    row_copy(left_b, d, False).wait_recv()
                    outgoing[left_b, d] = (
                        part[left_b, d] + from_right[left_b, d].astype(F32)
                    ).astype(BF16)
                    row_copy(left_b, d, False).start()

    def stage(s, carry):
        @pl.when(s + AHEAD < nb)
        def _():
            own_start(s + AHEAD)

        @pl.when(s + 1 < nb)
        def _():
            take(s + 1, 1)

        block_step(s)
        flow_ends(s)

        @pl.when(s + 1 < nb)
        def _():
            for k in range(2, n_g):
                take(s + 1, k)

        @pl.when((s >= DELAY) & (s + 1 < nb))
        def _():
            flow_inner(s - DELAY)

        return carry

    lax.fori_loop(0, nb, stage, 0)

    def weight_grad(s, carry):
        made = lax.dot_general(routed[s], grads[...], BOTH, preferred_element_type=F32)
        at = pl.ds(pl.multiple_of(s * fw, fw), fw)
        sum_g[at, :] = made[:, :width]
        sum_u[at, :] = made[:, width:]
        return carry

    for s in range(n_g):
        weight_grad(s, 0)

    halves = (
        (sum_g, stage_g, got_g, order_g[::-1]),
        (sum_u, stage_u, got_u, order_u[::-1]),
    )

    def half_offset(phase):
        return sum(w_rows * 2 ** (n_bits - 1 - t) for t in range(phase))

    def half_copy(which, phase):
        total, stage_ref, got, order = halves[which]
        span = pl.ds(half_offset(phase), w_rows * 2 ** (n_bits - 1 - phase))
        return pltpu.make_async_remote_copy(
            src_ref=stage_ref.at[span],
            dst_ref=got.at[span],
            send_sem=h_send.at[which, phase],
            recv_sem=h_recv.at[which, phase],
            device_id={"dp": partner(order[phase])},
        )

    def half_places(which, phase, mine):
        order = halves[which][3]
        k = order[phase]
        rest = order[phase + 1 :]
        base = sum(bit(j) * 2**j for j in order[:phase])
        base = base + (bit(k) if mine else 1 - bit(k)) * 2**k
        start = half_offset(phase)
        for i in range(2 ** len(rest)):
            chunk = pl.multiple_of((base + scattered(rest, i)) * w_rows, w_rows)
            at = start + i * w_rows
            yield pl.ds(chunk, w_rows), slice(at, at + w_rows)

    def half_start(phase):
        for which in range(2):
            total, stage_ref, got, order = halves[which]
            for chunk, at in half_places(which, phase, False):
                stage_ref[at, :] = total[chunk, :].astype(BF16)
            half_copy(which, phase).start()

    def half_wait(phase):
        for which in range(2):
            total, stage_ref, got, order = halves[which]
            half_copy(which, phase).wait_recv()
            for chunk, at in half_places(which, phase, True):
                total[chunk, :] += got[at, :].astype(F32)

    half_start(0)
    steps = list(range(nb - 1 - DELAY, nb + HOP * (n_g - 3)))
    share = -(-len(steps) // max(n_bits - 1, 1))
    for phase in range(n_bits):
        half_wait(phase)
        if phase + 1 < n_bits:
            half_start(phase + 1)
        for step in steps[phase * share : (phase + 1) * share]:
            flow_inner(step)

    mine = pl.ds(pl.multiple_of(p * w_rows, w_rows), w_rows)
    grad_gate_w[...] = sum_g[mine, :] * factor
    grad_up_w[...] = sum_u[mine, :] * factor

    for b in range(nb):
        @pl.when(z > 0)
        def _():
            row_copy(b, z, True).wait_recv()

        @pl.when(z < n_g - 1)
        def _():
            row_copy(b, z, False).wait_recv()

        span = slice(b * blk, (b + 1) * blk)

        @pl.when(z == 0)
        def _():
            landed[span, :] = (part[b, z] + from_right[b, z].astype(F32)).astype(BF16)

        @pl.when(z == n_g - 1)
        def _():
            landed[span, :] = (part[b, z] + from_left[b, z].astype(F32)).astype(BF16)

        @pl.when((z > 0) & (z < n_g - 1))
        def _():
            landed[span, :] = (
                part[b, z] + from_left[b, z].astype(F32) + from_right[b, z].astype(F32)
            ).astype(BF16)

    tile = min(n_tok, 256)

    def place(t, carry):
        at = pl.ds(pl.multiple_of(t * tile, tile), tile)
        grad_tokens[at, :] = jnp.dot(
            onehot[at, :], landed[...], preferred_element_type=F32
        ).astype(BF16)
        return carry

    lax.fori_loop(0, n_tok // tile, place, 0)

    def drain(b, carry):
        @pl.when(z > 0)
        def _():
            own_left(b).wait_send()

        @pl.when(z < n_g - 1)
        def _():
            own_right(b).wait_send()

        for s in range(n_g):
            @pl.when(((s < z) & (z < n_g - 1)) | ((s > z) & (z > 0)))
            def _():
                feature_copy(s, b, fwd_sem.at[b, s], z).wait_send()

            @pl.when(s > z)
            def _():
                row_copy(b, s, True).wait_send()

            @pl.when(s < z)
            def _():
                row_copy(b, s, False).wait_send()

        return carry

    lax.fori_loop(0, nb, drain, 0)
    for phase in range(n_bits):
        for which in range(2):
            half_copy(which, phase).wait_send()


def store(*refs):
    sems = refs[-1]
    half = (len(refs) - 1) // 2
    copies = [
        pltpu.make_async_copy(refs[i], refs[half + i], sems.at[i]) for i in range(half)
    ]
    for copy in copies:
        copy.start()
    for copy in copies:
        copy.wait()


def shards(n_dp, n_g, tokens, gate_w, up_w, block_rows, block_count, route_gate, grad_hidden):
    n_blocks, block_len = block_rows.shape
    nb, blk = n_blocks * CUTS, block_len // CUTS
    n_tok, fw = tokens.shape
    w_rows, width = gate_w.shape
    routed_len = nb * blk
    depth = n_dp * w_rows
    n_bits = n_dp.bit_length() - 1
    factor = float((n_dp * routed_len) ** (-0.5))
    dma = pltpu.SemaphoreType.DMA
    vmem = pl.BlockSpec(memory_space=pltpu.VMEM)
    hbm = pl.BlockSpec(memory_space=pltpu.HBM)
    smem = pl.BlockSpec(memory_space=pltpu.SMEM)
    made = pl.pallas_call(
        functools.partial(kernel, n_dp, n_g, factor),
        out_shape=(
            jax.ShapeDtypeStruct((routed_len, width), BF16),
            jax.ShapeDtypeStruct((n_tok, fw), BF16),
            jax.ShapeDtypeStruct((w_rows, width), F32),
            jax.ShapeDtypeStruct((w_rows, width), F32),
        ),
        in_specs=[hbm, hbm, hbm, hbm, smem, hbm, hbm],
        out_specs=(vmem, vmem, vmem, vmem),
        scratch_shapes=[
            pltpu.VMEM((n_tok, fw), BF16),
            pltpu.VMEM((n_blocks, block_len), jnp.int32),
            pltpu.VMEM((n_blocks, block_len), F32),
            pltpu.VMEM((routed_len, width), BF16),
            pltpu.VMEM((n_tok, routed_len), BF16),
            pltpu.VMEM((routed_len, block_len), F32),
            pltpu.VMEM((n_g, routed_len, fw), BF16),
            pltpu.VMEM((depth, width), BF16),
            pltpu.VMEM((depth, width), BF16),
            pltpu.VMEM((routed_len, 2 * width), BF16),
            pltpu.VMEM((nb, n_g, blk, fw), F32),
            pltpu.VMEM((nb, n_g, blk, fw), BF16),
            pltpu.VMEM((nb, n_g, blk, fw), BF16),
            pltpu.VMEM((nb, n_g, blk, fw), BF16),
            pltpu.VMEM((routed_len, fw), BF16),
            pltpu.VMEM((depth, width), F32),
            pltpu.VMEM((depth, width), F32),
            pltpu.VMEM((depth, width), BF16),
            pltpu.VMEM((depth, width), BF16),
            pltpu.VMEM((depth, width), BF16),
            pltpu.VMEM((depth, width), BF16),
            dma((nb, 2)),
            dma((nb, n_g)),
            dma((nb, n_g)),
            dma((2, n_bits)),
            dma((2, n_bits)),
            dma((nb, n_g)),
            dma((nb, n_g)),
            dma((nb, n_g)),
            dma((2, n_bits)),
            dma((2, n_bits)),
            dma((6,)),
        ],
        compiler_params=pltpu.CompilerParams(
            collective_id=0, has_side_effects=True, vmem_limit_bytes=67043328
        ),
    )(tokens, gate_w, up_w, block_rows, block_count, route_gate, grad_hidden)
    return pl.pallas_call(
        store,
        out_shape=tuple(jax.ShapeDtypeStruct(x.shape, x.dtype) for x in made),
        in_specs=[vmem] * len(made),
        out_specs=(hbm,) * len(made),
        scratch_shapes=[dma((len(made),))],
        compiler_params=pltpu.CompilerParams(vmem_limit_bytes=2**20),
    )(*made)


def solution(mesh):
    return jax.shard_map(
        functools.partial(shards, mesh.shape["dp"], mesh.shape["group"]),
        mesh=mesh,
        in_specs=(
            P("dp", "group"),
            P("dp", "group"),
            P("dp", "group"),
            P("dp", None),
            P("dp"),
            P("dp", None),
            P("dp", "group"),
        ),
        out_specs=(P("dp", "group"), P("dp", "group"), P("dp", "group"), P("dp", "group")),
        check_vma=False,
    )
```

profile of v0, /device:TPU:0, one launch (start us, length us, event | category | flops | bytes accessed | tf_op | source)
XLA Modules:
  0.0 73.1 jit_solution(14212726267953932158)
XLA Ops:
  1.3 66.5 %shard_map.102 = (bf16[512,256]{1,0:T(8,128)(2,1)}, bf16[1024,512]{1,0:T(8,128)(2,1)}, f32[256,256]{1,0:T(8,128)}, f32[256,256]{1,0:T(8,128)}) custom-call(bf16[1024,512]{1,0:T(8,128)(2,1)} %tokens_in.1, bf16[256,256]{1,0:T(8,128)(2,1)} %gate_w.1, bf16[256,256]{1,0:T(8,128)(2,1)} %up_w.1, s32[4,128]{1,0:T(4,128)} %rows_in.1, s32[1]{0:T(128)S(6)} %copy.11.count, ...), custom_call_target="tpu_custom_call" | custom-call | tf_op jit(solution)/shard_map/pallas_call | solution.py:504
  67.8 0.0 copy-start
  67.8 1.2 %copy-done = bf16[1024,512]{1,0:T(8,128)(2,1)S(1)} copy-done((bf16[1024,512]{1,0:T(8,128)(2,1)S(1)}, bf16[1024,512]{1,0:T(8,128)(2,1)}, u32[]{:S(2)}) %copy-start) | copy-done | bytes 1048600
  69.0 0.0 copy-start.1
  69.0 0.9 %copy-done.1 = bf16[512,256]{1,0:T(8,128)(2,1)S(1)} copy-done((bf16[512,256]{1,0:T(8,128)(2,1)S(1)}, bf16[512,256]{1,0:T(8,128)(2,1)}, u32[]{:S(2)}) %copy-start.1) | copy-done | bytes 262168
  70.0 0.0 copy-start.2
  70.0 0.9 %copy-done.2 = f32[256,256]{1,0:T(8,128)S(1)} copy-done((f32[256,256]{1,0:T(8,128)S(1)}, f32[256,256]{1,0:T(8,128)}, u32[]{:S(2)}) %copy-start.2) | copy-done | bytes 262168
  70.9 0.0 copy-start.3
  70.9 0.9 %copy-done.3 = f32[256,256]{1,0:T(8,128)S(1)} copy-done((f32[256,256]{1,0:T(8,128)S(1)}, f32[256,256]{1,0:T(8,128)}, u32[]{:S(2)}) %copy-start.3) | copy-done | bytes 262168
  71.9 1.3 %shard_map.103 = (bf16[512,256]{1,0:T(8,128)(2,1)}, bf16[1024,512]{1,0:T(8,128)(2,1)}, f32[256,256]{1,0:T(8,128)}, f32[256,256]{1,0:T(8,128)}) custom-call(bf16[512,256]{1,0:T(8,128)(2,1)S(1)} %copy-done.1, bf16[1024,512]{1,0:T(8,128)(2,1)S(1)} %copy-done, f32[256,256]{1,0:T(8,128)S(1)} %copy-done.2, f32[256,256]{1,0:T(8,128)S(1)} %copy-done.3), custom_call_target="tpu_custom_call" | custom-call | tf_op jit(solution)/shard_map/pallas_call | solution.py:552
Async XLA Ops:
  67.8 1.2 %copy-start = (bf16[1024,512]{1,0:T(8,128)(2,1)S(1)}, bf16[1024,512]{1,0:T(8,128)(2,1)}, u32[]{:S(2)}) copy-start(bf16[1024,512]{1,0:T(8,128)(2,1)} %get-tuple-element.9.refs_1_) | copy-start | bytes 3145732
  69.0 0.9 %copy-start.1 = (bf16[512,256]{1,0:T(8,128)(2,1)S(1)}, bf16[512,256]{1,0:T(8,128)(2,1)}, u32[]{:S(2)}) copy-start(bf16[512,256]{1,0:T(8,128)(2,1)} %get-tuple-element.8.refs_0_) | copy-start | bytes 786436
  70.0 0.9 %copy-start.2 = (f32[256,256]{1,0:T(8,128)S(1)}, f32[256,256]{1,0:T(8,128)}, u32[]{:S(2)}) copy-start(f32[256,256]{1,0:T(8,128)} %get-tuple-element.10.refs_2_) | copy-start | bytes 786436
  70.9 0.9 %copy-start.3 = (f32[256,256]{1,0:T(8,128)S(1)}, f32[256,256]{1,0:T(8,128)}, u32[]{:S(2)}) copy-start(f32[256,256]{1,0:T(8,128)} %get-tuple-element.11.refs_3_) | copy-start | bytes 786436
where the time goes:
time: 73.4 us; the launch traced here: 73.1 us
  Pallas kernels  67.8 us (92%)
  local copies, waits for them, and re-layouts  4.07 us (6%)
  between operations  1.3 us (2%)
    pallas_call x1, Pallas kernels, shards(): pl.pallas_call(functools.partial(kernel, n_dp, n_g, factor), out_shape=(j...  66.5 us
    unnamed x8, local copies, waits for them, and re-layouts  4.07 us

commit v1 on v0

--- a/solution.py
+++ b/solution.py
@@ -501,13 +501,14 @@
     vmem = pl.BlockSpec(memory_space=pltpu.VMEM)
     hbm = pl.BlockSpec(memory_space=pltpu.HBM)
     smem = pl.BlockSpec(memory_space=pltpu.SMEM)
+    kept = routed_len * width * 2 + n_tok * fw * 2 + 2 * w_rows * width * 4
     made = pl.pallas_call(
         functools.partial(kernel, n_dp, n_g, factor),
         out_shape=(
-            jax.ShapeDtypeStruct((routed_len, width), BF16),
-            jax.ShapeDtypeStruct((n_tok, fw), BF16),
-            jax.ShapeDtypeStruct((w_rows, width), F32),
-            jax.ShapeDtypeStruct((w_rows, width), F32),
+            pltpu.VMEM((routed_len, width), BF16),
+            pltpu.VMEM((n_tok, fw), BF16),
+            pltpu.VMEM((w_rows, width), F32),
+            pltpu.VMEM((w_rows, width), F32),
         ),
         in_specs=[hbm, hbm, hbm, hbm, smem, hbm, hbm],
         out_specs=(vmem, vmem, vmem, vmem),
@@ -546,7 +547,7 @@
             dma((6,)),
         ],
         compiler_params=pltpu.CompilerParams(
-            collective_id=0, has_side_effects=True, vmem_limit_bytes=67043328
+            collective_id=0, has_side_effects=True, vmem_limit_bytes=67043328 - kept
         ),
     )(tokens, gate_w, up_w, block_rows, block_count, route_gate, grad_hidden)
     return pl.pallas_call(

time: 73.4 us -> 67.9 us (0.925)
  local copies, waits for them, and re-layouts: 4.07 us -> 0 us
  Pallas kernels: 67.8 us -> 66.5 us
    unnamed x8 -> x0, local copies, waits for them, and re-layouts: 4.07 us -> none
    pallas_call x1, Pallas kernels: 66.5 us -> 65.2 us  [shards(): pl.pallas_call(functools.partial(kernel, n_dp, n_g, factor), out_shape=(p...]
where the time goes in v1:
time: 67.9 us; the launch traced here: 67.8 us
  Pallas kernels  66.5 us (98%)
  between operations  1.29 us (2%)
    pallas_call x1, Pallas kernels, shards(): pl.pallas_call(functools.partial(kernel, n_dp, n_g, factor), out_shape=(p...  65.2 us

profile of v1, /device:TPU:0, one launch (start us, length us, event | category | flops | bytes accessed | tf_op | source)
XLA Modules:
  0.0 67.8 jit_solution(1669983811276749016)
XLA Ops:
  1.3 65.2 %shard_map.102 = (bf16[512,256]{1,0:T(8,128)(2,1)S(1)}, bf16[1024,512]{1,0:T(8,128)(2,1)S(1)}, f32[256,256]{1,0:T(8,128)S(1)}, f32[256,256]{1,0:T(8,128)S(1)}) custom-call(bf16[1024,512]{1,0:T(8,128)(2,1)} %tokens_in.1, bf16[256,256]{1,0:T(8,128)(2,1)} %gate_w.1, bf16[256,256]{1,0:T(8,128)(2,1)} %up_w.1, s32[4,128]{1,0:T(4,128)} %rows_in.1, ...), custom_call_target="tpu_custom_call" | custom-call | tf_op jit(solution)/shard_map/pallas_call | solution.py:505
  66.5 1.3 %shard_map.103 = (bf16[512,256]{1,0:T(8,128)(2,1)}, bf16[1024,512]{1,0:T(8,128)(2,1)}, f32[256,256]{1,0:T(8,128)}, f32[256,256]{1,0:T(8,128)}) custom-call(bf16[512,256]{1,0:T(8,128)(2,1)S(1)} %get-tuple-element.8.refs_0_, bf16[1024,512]{1,0:T(8,128)(2,1)S(1)} %get-tuple-element.9.refs_1_, f32[256,256]{1,0:T(8,128)S(1)} %get-tuple-element.10.refs_2_, ...), custom_call_target="tpu_custom_call" | custom-call | tf_op jit(solution)/shard_map/pallas_call | solution.py:553

commit v2 on v1

--- a/solution.py
+++ b/solution.py
@@ -9,16 +9,14 @@
 
 F32 = jnp.float32
 BF16 = jnp.bfloat16
-CUTS = 1
+CUTS = 2
 AHEAD = 3
-HOP = 1
-DELAY = 1
+NEAR = 2
+LEAD = 3
+HOP = 2
+DEFER = 4
 BOTH = (((0,), (0,)), ((), ()))
 BACK = (((1,), (1,)), ((), ()))
-
-
-def scattered(bits, number):
-    return sum(((number >> at) & 1) << bit for at, bit in enumerate(bits))
 
 
 def kernel(
@@ -84,8 +82,11 @@
         return p + 2**k - bit(k) * 2 ** (k + 1)
 
     upper = list(range(1, n_bits))
-    order_g = upper + [0]
-    order_u = upper[::-1] + [0]
+    orders = (upper + [0], upper[::-1] + [0])
+    inner = (z > 0) & (z < n_g - 1)
+
+    def flipped(bits):
+        return p + sum((1 - 2 * bit(k)) * 2**k for k in bits)
 
     copies_in = [
         pltpu.make_async_copy(source, dest, local_sem.at[i])
@@ -129,43 +130,41 @@
     sides = jnp.minimum(z, 1) + jnp.minimum(n_g - 1 - z, 1)
     pl.semaphore_wait(barrier, n_bits + sides)
 
-    def weight_copies(which, phase):
-        source, dest, order = ((gate_w, wg, order_g), (up_w, wu, order_u))[which]
-        k = order[phase]
-        done = order[:phase]
-        base = p - sum(bit(j) * 2**j for j in done) if done else p
-        copies = []
-        for i in range(2**phase):
-            c = base + scattered(done, i)
-            place = dest.at[pl.ds(c * w_rows, w_rows)]
-            copies.append(
-                pltpu.make_async_remote_copy(
-                    src_ref=source if phase == 0 else place,
-                    dst_ref=dest.at[pl.ds(p * w_rows, w_rows)] if phase == 0 else place,
-                    send_sem=w_send.at[which, phase],
-                    recv_sem=w_recv.at[which, phase],
-                    device_id={"dp": partner(k)},
-                )
-            )
-        return copies
-
-    def weight_start(phase):
+    def weight_copy(which, phase, group, owner):
+        source, dest = ((gate_w, wg), (up_w, wu))[which]
+        place = dest.at[pl.ds(pl.multiple_of(owner * w_rows, w_rows), w_rows)]
+        return pltpu.make_async_remote_copy(
+            src_ref=place if group else source,
+            dst_ref=place,
+            send_sem=w_send.at[which, phase, group],
+            recv_sem=w_recv.at[which, phase, group],
+            device_id={"dp": partner(orders[which][phase])},
+        )
+
+    def weight_whole(which, phase, group):
+        span = (wg, wu)[which].at[pl.ds(0, w_rows * (2 ** (group - 1) if group else 1))]
+        return pltpu.make_async_remote_copy(
+            src_ref=span,
+            dst_ref=span,
+            send_sem=w_send.at[which, phase, group],
+            recv_sem=w_recv.at[which, phase, group],
+            device_id={"dp": partner(orders[which][phase])},
+        )
+
+    def weight_own(phase):
         for which in range(2):
-            for copy in weight_copies(which, phase):
-                copy.start()
-
-    def weight_wait(phase):
+            weight_copy(which, phase, 0, p).start()
+
+    def weight_pass(phase, group):
         for which in range(2):
-            dest, order = ((wg, order_g), (wu, order_u))[which]
-            span = dest.at[pl.ds(0, w_rows * 2**phase)]
-            whole = pltpu.make_async_remote_copy(
-                src_ref=span,
-                dst_ref=span,
-                send_sem=w_send.at[which, phase],
-                recv_sem=w_recv.at[which, phase],
-                device_id={"dp": partner(order[phase])},
-            )
-            whole.wait()
+            order = orders[which]
+            weight_whole(which, phase, group).wait_recv()
+            low = order[: group - 1] if group else []
+            for later in range(phase + 1, n_bits):
+                for number in range(2 ** len(low)):
+                    bits = [order[phase]] + ([order[group - 1]] if group else [])
+                    bits += [k for at, k in enumerate(low) if (number >> at) & 1]
+                    weight_copy(which, later, phase + 1, flipped(bits)).start()
 
     def feature_copy(s, b, send_sem, to):
         place = routed.at[s, pl.ds(pl.multiple_of(b * blk, blk), blk)]
@@ -209,14 +208,35 @@
             def _():
                 feature_copy(z + k, b, fwd_sem.at[b, z + k], z - 1).start()
 
-    weight_start(0)
+    def gather(b):
+        @pl.when(b + AHEAD < nb)
+        def _():
+            own_start(b + AHEAD)
+
+        @pl.when(b + NEAR < nb)
+        def _():
+            take(b + NEAR, 1)
+
+        for k in range(2, n_g):
+            take(b, k)
+
     cuts = block_len // blk
-    for b in range(min(AHEAD, cuts)):
-        own_start(b)
+
+    def own_block(b):
+        for at in range(b * cuts, (b + 1) * cuts):
+            if at < AHEAD:
+                own_start(at)
+            else:
+                @pl.when(jnp.logical_not(inner))
+                def _():
+                    own_start(at)
+
+    own_block(0)
+    for phase in range(n_bits):
+        weight_own(phase)
     for b in range(1, n_blocks):
         pick(b)
-        for at in range(b * cuts, min(AHEAD, (b + 1) * cuts)):
-            own_start(at)
+        own_block(b)
     copies_in[2].wait()
     live = lax.broadcasted_iota(jnp.int32, (n_blocks, block_len), 0) < count[0]
     weights = jnp.where(live, route[...], 0.0)
@@ -226,16 +246,23 @@
     for copy in copies_in[3:]:
         copy.wait()
 
-    distance = 1
-    for phase in range(n_bits):
-        weight_wait(phase)
-        if phase + 1 < n_bits:
-            weight_start(phase + 1)
-        if distance < n_g:
-            take(0, distance)
-            distance += 1
-    for k in range(distance, n_g):
-        take(0, k)
+    groups = [(phase, group) for phase in range(n_bits) for group in range(phase + 1)]
+
+    @pl.when(inner)
+    def _():
+        for b in range(NEAR):
+            take(b, 1)
+
+    early = [pair for pair in groups if pair[0] < n_bits - 1]
+    for at, (phase, group) in enumerate(early):
+        weight_pass(phase, group)
+        for b in range(at * LEAD // len(early), (at + 1) * LEAD // len(early)):
+            @pl.when(inner)
+            def _():
+                gather(b)
+
+    for phase, group in groups[len(early) :]:
+        weight_pass(phase, group)
 
     def block_step(b):
         span = pl.ds(pl.multiple_of(b * blk, blk), blk)
@@ -272,23 +299,34 @@
             device_id={"group": z + 1 if right else z - 1},
         )
 
-    def flow_ends(b):
+    def end_send(b, d, right):
+        outgoing[b, d] = part[b, d].astype(BF16)
+        row_copy(b, d, right).start()
+
+    def flow_far(b):
         @pl.when(z == 0)
         def _():
-            for d in range(n_g - 1, 0, -1):
-                outgoing[b, d] = part[b, d].astype(BF16)
-                row_copy(b, d, True).start()
+            for d in range(n_g - 1, 1, -1):
+                end_send(b, d, True)
 
         @pl.when(z == n_g - 1)
         def _():
-            for d in range(n_g - 1):
-                outgoing[b, d] = part[b, d].astype(BF16)
-                row_copy(b, d, False).start()
+            for d in range(n_g - 2):
+                end_send(b, d, False)
+
+    def flow_near(b):
+        @pl.when(z == 0)
+        def _():
+            end_send(b, 1, True)
+
+        @pl.when(z == n_g - 1)
+        def _():
+            end_send(b, n_g - 2, False)
 
     def flow_inner(s):
         right_b = s - HOP * (z - 1)
 
-        @pl.when((z > 0) & (z < n_g - 1) & (right_b >= 0) & (right_b < nb))
+        @pl.when(inner & (right_b >= 0) & (right_b < nb))
         def _():
             for k in range(n_g - 1, 0, -1):
                 d = z + k
@@ -303,7 +341,7 @@
 
         left_b = s - HOP * (n_g - 2 - z)
 
-        @pl.when((z > 0) & (z < n_g - 1) & (left_b >= 0) & (left_b < nb))
+        @pl.when(inner & (left_b >= 0) & (left_b < nb))
         def _():
             for k in range(n_g - 1, 0, -1):
                 d = z - k
@@ -316,99 +354,136 @@
                     ).astype(BF16)
                     row_copy(left_b, d, False).start()
 
+    begin = nb - 1 - LEAD
+
     def stage(s, carry):
-        @pl.when(s + AHEAD < nb)
-        def _():
-            own_start(s + AHEAD)
-
-        @pl.when(s + 1 < nb)
-        def _():
-            take(s + 1, 1)
+        @pl.when(inner & (s + LEAD < nb))
+        def _():
+            gather(s + LEAD)
+
+        @pl.when(jnp.logical_not(inner))
+        def _():
+            for k in range(1, n_g):
+                take(s, k)
 
         block_step(s)
-        flow_ends(s)
-
-        @pl.when(s + 1 < nb)
-        def _():
-            for k in range(2, n_g):
-                take(s + 1, k)
-
-        @pl.when((s >= DELAY) & (s + 1 < nb))
-        def _():
-            flow_inner(s - DELAY)
+        flow_far(s)
+
+        @pl.when(s >= DEFER)
+        def _():
+            flow_near(s - DEFER)
+
+        @pl.when(s >= begin)
+        def _():
+            flow_inner(s - begin)
 
         return carry
 
     lax.fori_loop(0, nb, stage, 0)
-
-    def weight_grad(s, carry):
-        made = lax.dot_general(routed[s], grads[...], BOTH, preferred_element_type=F32)
-        at = pl.ds(pl.multiple_of(s * fw, fw), fw)
-        sum_g[at, :] = made[:, :width]
-        sum_u[at, :] = made[:, width:]
-        return carry
-
-    for s in range(n_g):
-        weight_grad(s, 0)
-
-    halves = (
-        (sum_g, stage_g, got_g, order_g[::-1]),
-        (sum_u, stage_u, got_u, order_u[::-1]),
-    )
-
-    def half_offset(phase):
-        return sum(w_rows * 2 ** (n_bits - 1 - t) for t in range(phase))
-
-    def half_copy(which, phase):
-        total, stage_ref, got, order = halves[which]
-        span = pl.ds(half_offset(phase), w_rows * 2 ** (n_bits - 1 - phase))
+    for b in range(nb - DEFER, nb):
+        flow_near(b)
+
+    totals = ((sum_g, stage_g, got_g), (sum_u, stage_u, got_u))
+    paths = [order[::-1] for order in orders]
+    small = w_rows % 128 > 0
+
+    def weight_grad(which, owner):
+        total = totals[which][0]
+        chunk = pl.ds(pl.multiple_of(owner * w_rows, w_rows), w_rows)
+        if small:
+            return total[chunk, :]
+        per = fw // w_rows
+        across = pl.ds(pl.multiple_of((owner % per) * w_rows, w_rows), w_rows)
+        return lax.dot_general(
+            routed[owner // per, :, across],
+            grads[:, which * width : (which + 1) * width],
+            BOTH,
+            preferred_element_type=F32,
+        )
+
+    def half_count(phase):
+        return 2 ** max(n_bits - 2 - phase, 0)
+
+    def half_sides(phase):
+        return range(2 if phase < n_bits - 1 else 1)
+
+    def half_at(phase, side, i):
+        start = sum(2 ** (n_bits - 1 - t) for t in range(phase))
+        at = (start + side * half_count(phase) + i) * w_rows
+        return slice(at, at + w_rows)
+
+    def half_owner(which, phase, side, i, mine):
+        path = paths[which]
+        bits = [] if mine else [path[phase]]
+        if phase < n_bits - 1 and side == 0:
+            bits.append(path[phase + 1])
+        bits += [k for at, k in enumerate(path[phase + 2 :]) if (i >> at) & 1]
+        return flipped(bits)
+
+    def half_copy(which, phase, side):
+        total, stage_ref, got = totals[which]
+        at = half_at(phase, side, 0).start
+        span = pl.ds(at, half_count(phase) * w_rows)
         return pltpu.make_async_remote_copy(
             src_ref=stage_ref.at[span],
             dst_ref=got.at[span],
-            send_sem=h_send.at[which, phase],
-            recv_sem=h_recv.at[which, phase],
-            device_id={"dp": partner(order[phase])},
+            send_sem=h_send.at[which, phase, side],
+            recv_sem=h_recv.at[which, phase, side],
+            device_id={"dp": partner(paths[which][phase])},
         )
 
-    def half_places(which, phase, mine):
-        order = halves[which][3]
-        k = order[phase]
-        rest = order[phase + 1 :]
-        base = sum(bit(j) * 2**j for j in order[:phase])
-        base = base + (bit(k) if mine else 1 - bit(k)) * 2**k
-        start = half_offset(phase)
-        for i in range(2 ** len(rest)):
-            chunk = pl.multiple_of((base + scattered(rest, i)) * w_rows, w_rows)
-            at = start + i * w_rows
-            yield pl.ds(chunk, w_rows), slice(at, at + w_rows)
-
-    def half_start(phase):
+    def half_begin():
+        if small:
+            for s in range(n_g):
+                made = lax.dot_general(
+                    routed[s], grads[...], BOTH, preferred_element_type=F32
+                )
+                sum_g[s * fw : (s + 1) * fw, :] = made[:, :width]
+                sum_u[s * fw : (s + 1) * fw, :] = made[:, width:]
+        for side in half_sides(0):
+            for which in range(2):
+                for i in range(half_count(0)):
+                    made = weight_grad(which, half_owner(which, 0, side, i, False))
+                    totals[which][1][half_at(0, side, i), :] = made.astype(BF16)
+                half_copy(which, 0, side).start()
+        if not small:
+            for side in half_sides(0):
+                for which in range(2):
+                    for i in range(half_count(0)):
+                        owner = half_owner(which, 0, side, i, True)
+                        chunk = pl.ds(pl.multiple_of(owner * w_rows, w_rows), w_rows)
+                        totals[which][0][chunk, :] = weight_grad(which, owner)
+
+    def half_pass(phase, side):
         for which in range(2):
-            total, stage_ref, got, order = halves[which]
-            for chunk, at in half_places(which, phase, False):
-                stage_ref[at, :] = total[chunk, :].astype(BF16)
-            half_copy(which, phase).start()
-
-    def half_wait(phase):
-        for which in range(2):
-            total, stage_ref, got, order = halves[which]
-            half_copy(which, phase).wait_recv()
-            for chunk, at in half_places(which, phase, True):
-                total[chunk, :] += got[at, :].astype(F32)
-
-    half_start(0)
-    steps = list(range(nb - 1 - DELAY, nb + HOP * (n_g - 3)))
-    share = -(-len(steps) // max(n_bits - 1, 1))
+            total, stage_ref, got = totals[which]
+            half_copy(which, phase, side).wait_recv()
+            for i in range(half_count(phase)):
+                owner = half_owner(which, phase, side, i, True)
+                chunk = pl.ds(pl.multiple_of(owner * w_rows, w_rows), w_rows)
+                value = total[chunk, :] + got[half_at(phase, side, i), :].astype(F32)
+                if phase == n_bits - 1:
+                    (grad_gate_w, grad_up_w)[which][...] = value * factor
+                elif side == 1:
+                    total[chunk, :] = value
+                elif phase == n_bits - 2:
+                    stage_ref[half_at(phase + 1, 0, 0), :] = value.astype(BF16)
+                else:
+                    at = half_at(phase + 1, 1 - i % 2, i // 2)
+                    stage_ref[at, :] = value.astype(BF16)
+            if phase < n_bits - 1 and side == 0:
+                for later in half_sides(phase + 1):
+                    half_copy(which, phase + 1, later).start()
+
+    half_begin()
+    steps = list(range(nb - begin, nb + HOP * (n_g - 3)))
     for phase in range(n_bits):
-        half_wait(phase)
-        if phase + 1 < n_bits:
-            half_start(phase + 1)
-        for step in steps[phase * share : (phase + 1) * share]:
+        for step in steps[phase : phase + 1]:
             flow_inner(step)
-
-    mine = pl.ds(pl.multiple_of(p * w_rows, w_rows), w_rows)
-    grad_gate_w[...] = sum_g[mine, :] * factor
-    grad_up_w[...] = sum_u[mine, :] * factor
+        for side in half_sides(phase):
+            half_pass(phase, side)
+    for step in steps[n_bits:]:
+        flow_inner(step)
 
     for b in range(nb):
         @pl.when(z > 0)
@@ -429,7 +504,7 @@
         def _():
             landed[span, :] = (part[b, z] + from_left[b, z].astype(F32)).astype(BF16)
 
-        @pl.when((z > 0) & (z < n_g - 1))
+        @pl.when(inner)
         def _():
             landed[span, :] = (
                 part[b, z] + from_left[b, z].astype(F32) + from_right[b, z].astype(F32)
@@ -471,9 +546,12 @@
         return carry
 
     lax.fori_loop(0, nb, drain, 0)
-    for phase in range(n_bits):
-        for which in range(2):
-            half_copy(which, phase).wait_send()
+    for which in range(2):
+        for phase, group in groups:
+            weight_whole(which, phase, group).wait_send()
+        for phase in range(n_bits):
+            for side in half_sides(phase):
+                half_copy(which, phase, side).wait_send()
 
 
 def store(*refs):
@@ -537,13 +615,13 @@
             dma((nb, 2)),
             dma((nb, n_g)),
             dma((nb, n_g)),
-            dma((2, n_bits)),
-            dma((2, n_bits)),
+            dma((2, n_bits, n_bits)),
+            dma((2, n_bits, n_bits)),
             dma((nb, n_g)),
             dma((nb, n_g)),
             dma((nb, n_g)),
-            dma((2, n_bits)),
-            dma((2, n_bits)),
+            dma((2, n_bits, 2)),
+            dma((2, n_bits, 2)),
             dma((6,)),
         ],
         compiler_params=pltpu.CompilerParams(

time: 67.9 us -> 65.2 us (0.960)
  Pallas kernels: 66.5 us -> 63.8 us
    pallas_call x1, Pallas kernels: 65.2 us -> 62.5 us  [shards(): pl.pallas_call(functools.partial(kernel, n_dp, n_g, factor), out_shape=(p...]
where the time goes in v2:
time: 65.2 us; the launch traced here: 65.1 us
  Pallas kernels  63.8 us (98%)
  between operations  1.29 us (2%)
    pallas_call x1, Pallas kernels, shards(): pl.pallas_call(functools.partial(kernel, n_dp, n_g, factor), out_shape=(p...  62.5 us

profile of v2, /device:TPU:0, one launch (start us, length us, event | category | flops | bytes accessed | tf_op | source)
XLA Modules:
  0.0 65.1 jit_solution(15154415960191089498)
XLA Ops:
  1.3 62.5 %shard_map.102 = (bf16[512,256]{1,0:T(8,128)(2,1)S(1)}, bf16[1024,512]{1,0:T(8,128)(2,1)S(1)}, f32[256,256]{1,0:T(8,128)S(1)}, f32[256,256]{1,0:T(8,128)S(1)}) custom-call(bf16[1024,512]{1,0:T(8,128)(2,1)} %tokens_in.1, bf16[256,256]{1,0:T(8,128)(2,1)} %gate_w.1, bf16[256,256]{1,0:T(8,128)(2,1)} %up_w.1, s32[4,128]{1,0:T(4,128)} %rows_in.1, ...), custom_call_target="tpu_custom_call" | custom-call | tf_op jit(solution)/shard_map/pallas_call | solution.py:583
  63.8 1.3 %shard_map.103 = (bf16[512,256]{1,0:T(8,128)(2,1)}, bf16[1024,512]{1,0:T(8,128)(2,1)}, f32[256,256]{1,0:T(8,128)}, f32[256,256]{1,0:T(8,128)}) custom-call(bf16[512,256]{1,0:T(8,128)(2,1)S(1)} %get-tuple-element.8.refs_0_, bf16[1024,512]{1,0:T(8,128)(2,1)S(1)} %get-tuple-element.9.refs_1_, f32[256,256]{1,0:T(8,128)S(1)} %get-tuple-element.10.refs_2_, ...), custom_call_target="tpu_custom_call" | custom-call | tf_op jit(solution)/shard_map/pallas_call | solution.py:631

commit v3 on v2

--- a/solution.py
+++ b/solution.py
@@ -10,11 +10,13 @@
 F32 = jnp.float32
 BF16 = jnp.bfloat16
 CUTS = 2
-AHEAD = 3
+AHEAD = 4
 NEAR = 2
-LEAD = 3
+LEAD = 2
 HOP = 2
-DEFER = 4
+LATE = 4
+LAST = 2
+EARLY = 0
 BOTH = (((0,), (0,)), ((), ()))
 BACK = (((1,), (1,)), ((), ()))
 
@@ -323,38 +325,39 @@
         def _():
             end_send(b, n_g - 2, False)
 
+    def relay(b, d, right):
+        row_copy(b, d, right).wait_recv()
+        come = (from_left if right else from_right)[b, d]
+        outgoing[b, d] = (part[b, d] + come.astype(F32)).astype(BF16)
+        row_copy(b, d, right).start()
+
+    def flow_side(b, right):
+        final = n_g - 1 if right else 0
+
+        @pl.when(inner & (b >= 0) & (b < nb))
+        def _():
+            for k in range(n_g - 1, 0, -1):
+                d = z + k if right else z - k
+                go = (d < n_g) if right else (d >= 0)
+                if k == 1:
+                    go = go & ((d == final) | (b < nb - LAST))
+
+                @pl.when(go)
+                def _():
+                    relay(b, d, right)
+
+        d = z + 1 if right else z - 1
+
+        @pl.when(inner & (b == nb - 1) & (d != final))
+        def _():
+            for late in range(nb - LAST, nb):
+                relay(late, d, right)
+
     def flow_inner(s):
-        right_b = s - HOP * (z - 1)
-
-        @pl.when(inner & (right_b >= 0) & (right_b < nb))
-        def _():
-            for k in range(n_g - 1, 0, -1):
-                d = z + k
-
-                @pl.when(d < n_g)
-                def _():
-                    row_copy(right_b, d, True).wait_recv()
-                    outgoing[right_b, d] = (
-                        part[right_b, d] + from_left[right_b, d].astype(F32)
-                    ).astype(BF16)
-                    row_copy(right_b, d, True).start()
-
-        left_b = s - HOP * (n_g - 2 - z)
-
-        @pl.when(inner & (left_b >= 0) & (left_b < nb))
-        def _():
-            for k in range(n_g - 1, 0, -1):
-                d = z - k
-
-                @pl.when(d >= 0)
-                def _():
-                    row_copy(left_b, d, False).wait_recv()
-                    outgoing[left_b, d] = (
-                        part[left_b, d] + from_right[left_b, d].astype(F32)
-                    ).astype(BF16)
-                    row_copy(left_b, d, False).start()
-
-    begin = nb - 1 - LEAD
+        flow_side(s - HOP * (z - 1), True)
+        flow_side(s - HOP * (n_g - 2 - z), False)
+
+    begin = nb - 1 - LEAD - EARLY
 
     def stage(s, carry):
         @pl.when(inner & (s + LEAD < nb))
@@ -366,21 +369,21 @@
             for k in range(1, n_g):
                 take(s, k)
 
+        @pl.when(s >= begin)
+        def _():
+            flow_inner(s - begin)
+
         block_step(s)
         flow_far(s)
 
-        @pl.when(s >= DEFER)
-        def _():
-            flow_near(s - DEFER)
-
-        @pl.when(s >= begin)
-        def _():
-            flow_inner(s - begin)
+        @pl.when(s < nb - LATE)
+        def _():
+            flow_near(s)
 
         return carry
 
     lax.fori_loop(0, nb, stage, 0)
-    for b in range(nb - DEFER, nb):
+    for b in range(nb - LATE, nb):
         flow_near(b)
 
     totals = ((sum_g, stage_g, got_g), (sum_u, stage_u, got_u))
@@ -401,36 +404,55 @@
             preferred_element_type=F32,
         )
 
+    def half_groups(phase):
+        if phase < n_bits - 2:
+            return [(0, 1), (0, 0), (1, 1), (1, 0)]
+        return [(0, 0), (1, 0)] if phase == n_bits - 2 else [(0, 0)]
+
     def half_count(phase):
-        return 2 ** max(n_bits - 2 - phase, 0)
-
-    def half_sides(phase):
-        return range(2 if phase < n_bits - 1 else 1)
-
-    def half_at(phase, side, i):
+        return 2 ** max(n_bits - 3 - phase, 0)
+
+    def half_at(phase, group, i):
         start = sum(2 ** (n_bits - 1 - t) for t in range(phase))
-        at = (start + side * half_count(phase) + i) * w_rows
-        return slice(at, at + w_rows)
-
-    def half_owner(which, phase, side, i, mine):
+        at = start + half_groups(phase).index(group) * half_count(phase) + i
+        return slice(at * w_rows, (at + 1) * w_rows)
+
+    def half_owner(which, phase, group, i, mine):
         path = paths[which]
         bits = [] if mine else [path[phase]]
-        if phase < n_bits - 1 and side == 0:
+        if phase < n_bits - 1 and group[0] == 0:
             bits.append(path[phase + 1])
-        bits += [k for at, k in enumerate(path[phase + 2 :]) if (i >> at) & 1]
+        if phase < n_bits - 2 and group[1] == 1:
+            bits.append(path[phase + 2])
+        bits += [k for at, k in enumerate(path[phase + 3 :]) if (i >> at) & 1]
         return flipped(bits)
 
-    def half_copy(which, phase, side):
+    def half_copy(which, phase, group):
         total, stage_ref, got = totals[which]
-        at = half_at(phase, side, 0).start
+        at = half_at(phase, group, 0).start
         span = pl.ds(at, half_count(phase) * w_rows)
+        number = half_groups(phase).index(group)
         return pltpu.make_async_remote_copy(
             src_ref=stage_ref.at[span],
             dst_ref=got.at[span],
-            send_sem=h_send.at[which, phase, side],
-            recv_sem=h_recv.at[which, phase, side],
+            send_sem=h_send.at[which, phase, number],
+            recv_sem=h_recv.at[which, phase, number],
             device_id={"dp": partner(paths[which][phase])},
         )
+
+    def half_first(group):
+        for which in range(2):
+            for i in range(half_count(0)):
+                made = weight_grad(which, half_owner(which, 0, group, i, False))
+                totals[which][1][half_at(0, group, i), :] = made.astype(BF16)
+            half_copy(which, 0, group).start()
+
+    def half_keep(group):
+        for which in range(2):
+            for i in range(half_count(0)):
+                owner = half_owner(which, 0, group, i, True)
+                chunk = pl.ds(pl.multiple_of(owner * w_rows, w_rows), w_rows)
+                totals[which][0][chunk, :] = weight_grad(which, owner)
 
     def half_begin():
         if small:
@@ -440,48 +462,48 @@
                 )
                 sum_g[s * fw : (s + 1) * fw, :] = made[:, :width]
                 sum_u[s * fw : (s + 1) * fw, :] = made[:, width:]
-        for side in half_sides(0):
-            for which in range(2):
-                for i in range(half_count(0)):
-                    made = weight_grad(which, half_owner(which, 0, side, i, False))
-                    totals[which][1][half_at(0, side, i), :] = made.astype(BF16)
-                half_copy(which, 0, side).start()
-        if not small:
-            for side in half_sides(0):
-                for which in range(2):
-                    for i in range(half_count(0)):
-                        owner = half_owner(which, 0, side, i, True)
-                        chunk = pl.ds(pl.multiple_of(owner * w_rows, w_rows), w_rows)
-                        totals[which][0][chunk, :] = weight_grad(which, owner)
-
-    def half_pass(phase, side):
+        todo = half_groups(0)
+        half = max(len(todo) // 2, 1)
+        for group in todo[:half]:
+            half_first(group)
+        for group in todo[: 0 if small else half]:
+            half_keep(group)
+        for group in todo[half:]:
+            half_first(group)
+        for group in todo[0 if small else half : 0 if small else len(todo)]:
+            half_keep(group)
+
+    def half_pass(phase, group):
+        side, sub = group
+        after = 1 - sub if phase < n_bits - 2 else 0
         for which in range(2):
             total, stage_ref, got = totals[which]
-            half_copy(which, phase, side).wait_recv()
+            half_copy(which, phase, group).wait_recv()
             for i in range(half_count(phase)):
-                owner = half_owner(which, phase, side, i, True)
+                owner = half_owner(which, phase, group, i, True)
                 chunk = pl.ds(pl.multiple_of(owner * w_rows, w_rows), w_rows)
-                value = total[chunk, :] + got[half_at(phase, side, i), :].astype(F32)
+                value = total[chunk, :] + got[half_at(phase, group, i), :].astype(F32)
                 if phase == n_bits - 1:
                     (grad_gate_w, grad_up_w)[which][...] = value * factor
                 elif side == 1:
                     total[chunk, :] = value
-                elif phase == n_bits - 2:
-                    stage_ref[half_at(phase + 1, 0, 0), :] = value.astype(BF16)
+                elif phase + 1 < n_bits - 2:
+                    at = half_at(phase + 1, (after, i % 2), i // 2)
+                    stage_ref[at, :] = value.astype(BF16)
                 else:
-                    at = half_at(phase + 1, 1 - i % 2, i // 2)
-                    stage_ref[at, :] = value.astype(BF16)
+                    stage_ref[half_at(phase + 1, (after, 0), 0), :] = value.astype(BF16)
             if phase < n_bits - 1 and side == 0:
-                for later in half_sides(phase + 1):
-                    half_copy(which, phase + 1, later).start()
+                for later in half_groups(phase + 1):
+                    if phase == n_bits - 2 or later[0] == after:
+                        half_copy(which, phase + 1, later).start()
 
     half_begin()
     steps = list(range(nb - begin, nb + HOP * (n_g - 3)))
     for phase in range(n_bits):
         for step in steps[phase : phase + 1]:
             flow_inner(step)
-        for side in half_sides(phase):
-            half_pass(phase, side)
+        for group in half_groups(phase):
+            half_pass(phase, group)
     for step in steps[n_bits:]:
         flow_inner(step)
 
@@ -550,8 +572,8 @@
         for phase, group in groups:
             weight_whole(which, phase, group).wait_send()
         for phase in range(n_bits):
-            for side in half_sides(phase):
-                half_copy(which, phase, side).wait_send()
+            for group in half_groups(phase):
+                half_copy(which, phase, group).wait_send()
 
 
 def store(*refs):
@@ -620,8 +642,8 @@
             dma((nb, n_g)),
             dma((nb, n_g)),
             dma((nb, n_g)),
-            dma((2, n_bits, 2)),
-            dma((2, n_bits, 2)),
+            dma((2, n_bits, 4)),
+            dma((2, n_bits, 4)),
             dma((6,)),
         ],
         compiler_params=pltpu.CompilerParams(

time: 65.2 us -> 63.4 us (0.972)
  Pallas kernels: 63.8 us -> 62 us
    pallas_call x1, Pallas kernels: 62.5 us -> 60.7 us  [shards(): pl.pallas_call(functools.partial(kernel, n_dp, n_g, factor), out_shape=(p...]
where the time goes in v3:
time: 63.4 us; the launch traced here: 63.3 us
  Pallas kernels  62 us (98%)
  between operations  1.29 us (2%)
    pallas_call x1, Pallas kernels, shards(): pl.pallas_call(functools.partial(kernel, n_dp, n_g, factor), out_shape=(p...  60.7 us

profile of v3, /device:TPU:0, one launch (start us, length us, event | category | flops | bytes accessed | tf_op | source)
XLA Modules:
  0.0 63.3 jit_solution(13594112290704766176)
XLA Ops:
  1.3 60.7 %shard_map.102 = (bf16[512,256]{1,0:T(8,128)(2,1)S(1)}, bf16[1024,512]{1,0:T(8,128)(2,1)S(1)}, f32[256,256]{1,0:T(8,128)S(1)}, f32[256,256]{1,0:T(8,128)S(1)}) custom-call(bf16[1024,512]{1,0:T(8,128)(2,1)} %tokens_in.1, bf16[256,256]{1,0:T(8,128)(2,1)} %gate_w.1, bf16[256,256]{1,0:T(8,128)(2,1)} %up_w.1, s32[4,128]{1,0:T(4,128)} %rows_in.1, ...), custom_call_target="tpu_custom_call" | custom-call | tf_op jit(solution)/shard_map/pallas_call | solution.py:605
  62.0 1.3 %shard_map.103 = (bf16[512,256]{1,0:T(8,128)(2,1)}, bf16[1024,512]{1,0:T(8,128)(2,1)}, f32[256,256]{1,0:T(8,128)}, f32[256,256]{1,0:T(8,128)}) custom-call(bf16[512,256]{1,0:T(8,128)(2,1)S(1)} %get-tuple-element.8.refs_0_, bf16[1024,512]{1,0:T(8,128)(2,1)S(1)} %get-tuple-element.9.refs_1_, f32[256,256]{1,0:T(8,128)S(1)} %get-tuple-element.10.refs_2_, ...), custom_call_target="tpu_custom_call" | custom-call | tf_op jit(solution)/shard_map/pallas_call | solution.py:653

commit v4 on v3

--- a/solution.py
+++ b/solution.py
@@ -17,6 +17,9 @@
 LATE = 4
 LAST = 2
 EARLY = 0
+TILES = 4
+PRE = (1, 2)
+GO = (1, 2, 0)
 BOTH = (((0,), (0,)), ((), ()))
 BACK = (((1,), (1,)), ((), ()))
 
@@ -29,18 +32,19 @@
     gate_w,
     up_w,
     rows_in,
-    count,
+    count_in,
     route_in,
     grad_in,
     hidden,
-    grad_tokens,
     grad_gate_w,
     grad_up_w,
+    onehot,
+    landed,
     tokens,
     rows,
     route,
+    count,
     grad_hidden,
-    onehot,
     coef,
     routed,
     wg,
@@ -50,7 +54,6 @@
     outgoing,
     from_left,
     from_right,
-    landed,
     sum_g,
     sum_u,
     stage_g,
@@ -97,6 +100,7 @@
                 (tokens_in, tokens),
                 (rows_in, rows),
                 (route_in, route),
+                (count_in, count),
                 (gate_w, wg.at[pl.ds(p * w_rows, w_rows)]),
                 (up_w, wu.at[pl.ds(p * w_rows, w_rows)]),
                 (grad_in, grad_hidden),
@@ -211,16 +215,22 @@
                 feature_copy(z + k, b, fwd_sem.at[b, z + k], z - 1).start()
 
     def gather(b):
-        @pl.when(b + AHEAD < nb)
-        def _():
-            own_start(b + AHEAD)
-
-        @pl.when(b + NEAR < nb)
-        def _():
-            take(b + NEAR, 1)
-
-        for k in range(2, n_g):
-            take(b, k)
+        def own():
+            @pl.when(b + AHEAD < nb)
+            def _():
+                own_start(b + AHEAD)
+
+        def near():
+            @pl.when(b + NEAR < nb)
+            def _():
+                take(b + NEAR, 1)
+
+        def far():
+            for k in range(2, n_g):
+                take(b, k)
+
+        for which in GO:
+            (own, near, far)[which]()
 
     cuts = block_len // blk
 
@@ -240,12 +250,13 @@
         pick(b)
         own_block(b)
     copies_in[2].wait()
+    copies_in[3].wait()
     live = lax.broadcasted_iota(jnp.int32, (n_blocks, block_len), 0) < count[0]
     weights = jnp.where(live, route[...], 0.0)
     for b in range(n_blocks):
         turned = jnp.broadcast_to(weights[b : b + 1, :], (block_len, block_len)).T
         coef[b * block_len : (b + 1) * block_len, :] = turned
-    for copy in copies_in[3:]:
+    for copy in copies_in[4:]:
         copy.wait()
 
     groups = [(phase, group) for phase in range(n_bits) for group in range(phase + 1)]
@@ -258,15 +269,16 @@
     early = [pair for pair in groups if pair[0] < n_bits - 1]
     for at, (phase, group) in enumerate(early):
         weight_pass(phase, group)
-        for b in range(at * LEAD // len(early), (at + 1) * LEAD // len(early)):
-            @pl.when(inner)
-            def _():
-                gather(b)
+        for b in range(LEAD):
+            if PRE[b] == at:
+                @pl.when(inner)
+                def _():
+                    gather(b)
 
     for phase, group in groups[len(early) :]:
         weight_pass(phase, group)
 
-    def block_step(b):
+    def block_forward(b):
         span = pl.ds(pl.multiple_of(b * blk, blk), blk)
         gate = jnp.zeros((blk, width), F32)
         up = jnp.zeros((blk, width), F32)
@@ -283,14 +295,7 @@
         gu = (scaled * act).astype(BF16)
         grads[span, :width] = gg
         grads[span, width:] = gu
-        for d in range(n_g):
-            back = lax.dot_general(
-                gg, wg[d * fw : (d + 1) * fw, :], BACK, preferred_element_type=F32
-            )
-            back += lax.dot_general(
-                gu, wu[d * fw : (d + 1) * fw, :], BACK, preferred_element_type=F32
-            )
-            part[b, d] = back
+        return gg, gu
 
     def row_copy(b, d, right):
         return pltpu.make_async_remote_copy(
@@ -301,29 +306,33 @@
             device_id={"group": z + 1 if right else z - 1},
         )
 
-    def end_send(b, d, right):
-        outgoing[b, d] = part[b, d].astype(BF16)
-        row_copy(b, d, right).start()
-
-    def flow_far(b):
+    def end_start(b, d):
         @pl.when(z == 0)
         def _():
-            for d in range(n_g - 1, 1, -1):
-                end_send(b, d, True)
+            row_copy(b, d, True).start()
 
         @pl.when(z == n_g - 1)
         def _():
-            for d in range(n_g - 2):
-                end_send(b, d, False)
-
-    def flow_near(b):
-        @pl.when(z == 0)
-        def _():
-            end_send(b, 1, True)
-
-        @pl.when(z == n_g - 1)
-        def _():
-            end_send(b, n_g - 2, False)
+            row_copy(b, d, False).start()
+
+    def block_back(b, gg, gu):
+        for k in range(n_g):
+            d = jnp.where(2 * z < n_g, n_g - 1 - k, k)
+            place = pl.ds(pl.multiple_of(d * fw, fw), fw)
+            back = lax.dot_general(gg, wg[place, :], BACK, preferred_element_type=F32)
+            back += lax.dot_general(gu, wu[place, :], BACK, preferred_element_type=F32)
+            part[b, d] = back
+            if k < n_g - 1:
+                @pl.when(jnp.logical_not(inner))
+                def _():
+                    outgoing[b, d] = back.astype(BF16)
+
+            if k < n_g - 2:
+                end_start(b, d)
+            elif k == n_g - 2:
+                @pl.when(b < nb - LATE)
+                def _():
+                    end_start(b, d)
 
     def relay(b, d, right):
         row_copy(b, d, right).wait_recv()
@@ -359,7 +368,7 @@
 
     begin = nb - 1 - LEAD - EARLY
 
-    def stage(s, carry):
+    def arrive(s):
         @pl.when(inner & (s + LEAD < nb))
         def _():
             gather(s + LEAD)
@@ -373,18 +382,12 @@
         def _():
             flow_inner(s - begin)
 
-        block_step(s)
-        flow_far(s)
-
-        @pl.when(s < nb - LATE)
-        def _():
-            flow_near(s)
-
+    def stage(s, carry):
+        arrive(s)
+        block_back(s, *block_forward(s))
         return carry
 
-    lax.fori_loop(0, nb, stage, 0)
-    for b in range(nb - LATE, nb):
-        flow_near(b)
+    lax.fori_loop(0, nb - 1, stage, 0)
 
     totals = ((sum_g, stage_g, got_g), (sum_u, stage_u, got_u))
     paths = [order[::-1] for order in orders]
@@ -462,10 +465,10 @@
                 )
                 sum_g[s * fw : (s + 1) * fw, :] = made[:, :width]
                 sum_u[s * fw : (s + 1) * fw, :] = made[:, width:]
-        todo = half_groups(0)
-        half = max(len(todo) // 2, 1)
         for group in todo[:half]:
             half_first(group)
+
+    def half_rest():
         for group in todo[: 0 if small else half]:
             half_keep(group)
         for group in todo[half:]:
@@ -497,7 +500,15 @@
                     if phase == n_bits - 2 or later[0] == after:
                         half_copy(which, phase + 1, later).start()
 
+    todo = half_groups(0)
+    half = max(len(todo) // 2, 1)
+    arrive(nb - 1)
+    made = block_forward(nb - 1)
     half_begin()
+    block_back(nb - 1, *made)
+    for b in range(nb - LATE, nb):
+        end_start(b, jnp.where(z == 0, 1, n_g - 2))
+    half_rest()
     steps = list(range(nb - begin, nb + HOP * (n_g - 3)))
     for phase in range(n_bits):
         for step in steps[phase : phase + 1]:
@@ -532,17 +543,6 @@
                 part[b, z] + from_left[b, z].astype(F32) + from_right[b, z].astype(F32)
             ).astype(BF16)
 
-    tile = min(n_tok, 256)
-
-    def place(t, carry):
-        at = pl.ds(pl.multiple_of(t * tile, tile), tile)
-        grad_tokens[at, :] = jnp.dot(
-            onehot[at, :], landed[...], preferred_element_type=F32
-        ).astype(BF16)
-        return carry
-
-    lax.fori_loop(0, n_tok // tile, place, 0)
-
     def drain(b, carry):
         @pl.when(z > 0)
         def _():
@@ -576,14 +576,24 @@
                 half_copy(which, phase, group).wait_send()
 
 
-def store(*refs):
-    sems = refs[-1]
-    half = (len(refs) - 1) // 2
-    copies = [
-        pltpu.make_async_copy(refs[i], refs[half + i], sems.at[i]) for i in range(half)
-    ]
+def store(hidden, gate, up, onehot, landed, hidden_to, tokens_to, gate_to, up_to, made, sem):
+    n_tok = onehot.shape[0]
+    tile = n_tok // TILES
+    pairs = ((hidden, hidden_to), (gate, gate_to), (up, up_to))
+    copies = [pltpu.make_async_copy(*pair, sem.at[i]) for i, pair in enumerate(pairs)]
     for copy in copies:
         copy.start()
+    for t in range(TILES):
+        span = slice(t * tile, (t + 1) * tile)
+        made[span, :] = jnp.dot(
+            onehot[span, :], landed[...], preferred_element_type=F32
+        ).astype(BF16)
+        copies.append(
+            pltpu.make_async_copy(
+                made.at[span], tokens_to.at[span], sem.at[len(pairs) + t]
+            )
+        )
+        copies[-1].start()
     for copy in copies:
         copy.wait()
 
@@ -600,24 +610,25 @@
     dma = pltpu.SemaphoreType.DMA
     vmem = pl.BlockSpec(memory_space=pltpu.VMEM)
     hbm = pl.BlockSpec(memory_space=pltpu.HBM)
-    smem = pl.BlockSpec(memory_space=pltpu.SMEM)
-    kept = routed_len * width * 2 + n_tok * fw * 2 + 2 * w_rows * width * 4
+    outs = (
+        ((routed_len, width), BF16),
+        ((w_rows, width), F32),
+        ((w_rows, width), F32),
+        ((n_tok, routed_len), BF16),
+        ((routed_len, fw), BF16),
+    )
+    kept = sum(shape[0] * shape[1] * jnp.dtype(kind).itemsize for shape, kind in outs)
     made = pl.pallas_call(
         functools.partial(kernel, n_dp, n_g, factor),
-        out_shape=(
-            pltpu.VMEM((routed_len, width), BF16),
-            pltpu.VMEM((n_tok, fw), BF16),
-            pltpu.VMEM((w_rows, width), F32),
-            pltpu.VMEM((w_rows, width), F32),
-        ),
-        in_specs=[hbm, hbm, hbm, hbm, smem, hbm, hbm],
-        out_specs=(vmem, vmem, vmem, vmem),
+        out_shape=tuple(pltpu.VMEM(shape, kind) for shape, kind in outs),
+        in_specs=[hbm] * 7,
+        out_specs=(vmem,) * len(outs),
         scratch_shapes=[
             pltpu.VMEM((n_tok, fw), BF16),
             pltpu.VMEM((n_blocks, block_len), jnp.int32),
             pltpu.VMEM((n_blocks, block_len), F32),
+            pltpu.SMEM((1,), jnp.int32),
             pltpu.VMEM((routed_len, width), BF16),
-            pltpu.VMEM((n_tok, routed_len), BF16),
             pltpu.VMEM((routed_len, block_len), F32),
             pltpu.VMEM((n_g, routed_len, fw), BF16),
             pltpu.VMEM((depth, width), BF16),
@@ -627,7 +638,6 @@
             pltpu.VMEM((nb, n_g, blk, fw), BF16),
             pltpu.VMEM((nb, n_g, blk, fw), BF16),
             pltpu.VMEM((nb, n_g, blk, fw), BF16),
-            pltpu.VMEM((routed_len, fw), BF16),
             pltpu.VMEM((depth, width), F32),
             pltpu.VMEM((depth, width), F32),
             pltpu.VMEM((depth, width), BF16),
@@ -644,7 +654,7 @@
             dma((nb, n_g)),
             dma((2, n_bits, 4)),
             dma((2, n_bits, 4)),
-            dma((6,)),
+            dma((7,)),
         ],
         compiler_params=pltpu.CompilerParams(
             collective_id=0, has_side_effects=True, vmem_limit_bytes=67043328 - kept
@@ -652,11 +662,16 @@
     )(tokens, gate_w, up_w, block_rows, block_count, route_gate, grad_hidden)
     return pl.pallas_call(
         store,
-        out_shape=tuple(jax.ShapeDtypeStruct(x.shape, x.dtype) for x in made),
-        in_specs=[vmem] * len(made),
-        out_specs=(hbm,) * len(made),
-        scratch_shapes=[dma((len(made),))],
-        compiler_params=pltpu.CompilerParams(vmem_limit_bytes=2**20),
+        out_shape=(
+            jax.ShapeDtypeStruct((routed_len, width), BF16),
+            jax.ShapeDtypeStruct((n_tok, fw), BF16),
+            jax.ShapeDtypeStruct((w_rows, width), F32),
+            jax.ShapeDtypeStruct((w_rows, width), F32),
+        ),
+        in_specs=[vmem] * len(outs),
+        out_specs=(hbm,) * 4,
+        scratch_shapes=[pltpu.VMEM((n_tok, fw), BF16), dma((3 + TILES,))],
+        compiler_params=pltpu.CompilerParams(vmem_limit_bytes=8 * 2**20),
     )(*made)
 
 

time: 63.4 us -> 61.9 us (0.976)
  Pallas kernels: 62 us -> 60.4 us
    pallas_call x2, Pallas kernels: 62 us -> 60.4 us  [the longest x1 59 us: shards(): pl.pallas_call(functools.partial(kernel, n_dp, n_g, factor), out_shape=tu...]
where the time goes in v4:
time: 61.9 us; the launch traced here: 61.7 us
  Pallas kernels  60.4 us (98%)
  between operations  1.29 us (2%)
    pallas_call x1, Pallas kernels, shards(): pl.pallas_call(functools.partial(kernel, n_dp, n_g, factor), out_shape=tu...  59 us
    pallas_call x1, Pallas kernels, shards(): pl.pallas_call(store, out_shape=(jax.ShapeDtypeStruct((routed_len, width)...  1.48 us

profile of v4, /device:TPU:0, one launch (start us, length us, event | category | flops | bytes accessed | tf_op | source)
XLA Modules:
  0.0 61.7 jit_solution(4545140967438778821)
XLA Ops:
  1.3 59.0 %shard_map.102 = (bf16[512,256]{1,0:T(8,128)(2,1)S(1)}, f32[256,256]{1,0:T(8,128)S(1)}, f32[256,256]{1,0:T(8,128)S(1)}, bf16[1024,512]{1,0:T(8,128)(2,1)S(1)}, bf16[512,512]{1,0:T(8,128)(2,1)S(1)}) custom-call(bf16[1024,512]{1,0:T(8,128)(2,1)} %tokens_in.1, bf16[256,256]{1,0:T(8,128)(2,1)} %gate_w.1, bf16[256,256]{1,0:T(8,128)(2,1)} %up_w.1, ...), custom_call_target="tpu_custom_call" | custom-call | tf_op jit(solution)/shard_map/pallas_call | solution.py:621
  60.3 1.5 %shard_map.103 = (bf16[512,256]{1,0:T(8,128)(2,1)}, bf16[1024,512]{1,0:T(8,128)(2,1)}, f32[256,256]{1,0:T(8,128)}, f32[256,256]{1,0:T(8,128)}) custom-call(bf16[512,256]{1,0:T(8,128)(2,1)S(1)} %get-tuple-element.9.hidden, f32[256,256]{1,0:T(8,128)S(1)} %get-tuple-element.10.gate, f32[256,256]{1,0:T(8,128)S(1)} %get-tuple-element.11.up, ...), custom_call_target="tpu_custom_call" | custom-call | tf_op jit(solution)/shard_map/pallas_call | solution.py:663

commit v5 on v4

--- a/solution.py
+++ b/solution.py
@@ -18,6 +18,7 @@
 LAST = 2
 EARLY = 0
 TILES = 4
+FLOWS = (1,3,2)
 PRE = (1, 2)
 GO = (1, 2, 0)
 BOTH = (((0,), (0,)), ((), ()))
@@ -451,6 +452,8 @@
             half_copy(which, 0, group).start()
 
     def half_keep(group):
+        if small:
+            return
         for which in range(2):
             for i in range(half_count(0)):
                 owner = half_owner(which, 0, group, i, True)
@@ -467,14 +470,6 @@
                 sum_u[s * fw : (s + 1) * fw, :] = made[:, width:]
         for group in todo[:half]:
             half_first(group)
-
-    def half_rest():
-        for group in todo[: 0 if small else half]:
-            half_keep(group)
-        for group in todo[half:]:
-            half_first(group)
-        for group in todo[0 if small else half : 0 if small else len(todo)]:
-            half_keep(group)
 
     def half_pass(phase, group):
         side, sub = group
@@ -508,14 +503,25 @@
     block_back(nb - 1, *made)
     for b in range(nb - LATE, nb):
         end_start(b, jnp.where(z == 0, 1, n_g - 2))
-    half_rest()
     steps = list(range(nb - begin, nb + HOP * (n_g - 3)))
-    for phase in range(n_bits):
-        for step in steps[phase : phase + 1]:
+    done = [sum(FLOWS[: phase + 1]) for phase in range(n_bits)]
+    for step in steps[: done[0]]:
+        flow_inner(step)
+    for group in todo[:half]:
+        half_keep(group)
+        half_pass(0, group)
+    for group in todo[half:]:
+        half_first(group)
+    for group in todo[half:]:
+        half_keep(group)
+    for group in todo[half:]:
+        half_pass(0, group)
+    for phase in range(1, n_bits):
+        for step in steps[done[phase - 1] : done[phase]]:
             flow_inner(step)
         for group in half_groups(phase):
             half_pass(phase, group)
-    for step in steps[n_bits:]:
+    for step in steps[done[-1] :]:
         flow_inner(step)
 
     for b in range(nb):

time: 61.9 us -> 60.9 us (0.984)
  Pallas kernels: 60.4 us -> 59.5 us
    pallas_call x1, Pallas kernels: 59 us -> 58 us  [shards(): pl.pallas_call(functools.partial(kernel, n_dp, n_g, factor), out_shape=tu...]
where the time goes in v5:
time: 60.9 us; the launch traced here: 60.7 us
  Pallas kernels  59.5 us (98%)
  between operations  1.29 us (2%)
    pallas_call x1, Pallas kernels, shards(): pl.pallas_call(functools.partial(kernel, n_dp, n_g, factor), out_shape=tu...  58 us
    pallas_call x1, Pallas kernels, shards(): pl.pallas_call(store, out_shape=(jax.ShapeDtypeStruct((routed_len, width)...  1.48 us

profile of v5, /device:TPU:0, one launch (start us, length us, event | category | flops | bytes accessed | tf_op | source)
XLA Modules:
  0.0 60.7 jit_solution(14346081617256461689)
XLA Ops:
  1.3 58.0 %shard_map.102 = (bf16[512,256]{1,0:T(8,128)(2,1)S(1)}, f32[256,256]{1,0:T(8,128)S(1)}, f32[256,256]{1,0:T(8,128)S(1)}, bf16[1024,512]{1,0:T(8,128)(2,1)S(1)}, bf16[512,512]{1,0:T(8,128)(2,1)S(1)}) custom-call(bf16[1024,512]{1,0:T(8,128)(2,1)} %tokens_in.1, bf16[256,256]{1,0:T(8,128)(2,1)} %gate_w.1, bf16[256,256]{1,0:T(8,128)(2,1)} %up_w.1, ...), custom_call_target="tpu_custom_call" | custom-call | tf_op jit(solution)/shard_map/pallas_call | solution.py:627
  59.3 1.5 %shard_map.103 = (bf16[512,256]{1,0:T(8,128)(2,1)}, bf16[1024,512]{1,0:T(8,128)(2,1)}, f32[256,256]{1,0:T(8,128)}, f32[256,256]{1,0:T(8,128)}) custom-call(bf16[512,256]{1,0:T(8,128)(2,1)S(1)} %get-tuple-element.9.hidden, f32[256,256]{1,0:T(8,128)S(1)} %get-tuple-element.10.gate, f32[256,256]{1,0:T(8,128)S(1)} %get-tuple-element.11.up, ...), custom_call_target="tpu_custom_call" | custom-call | tf_op jit(solution)/shard_map/pallas_call | solution.py:669

commit v6 on v4

--- a/solution.py
+++ b/solution.py
@@ -15,10 +15,11 @@
 LEAD = 2
 HOP = 2
 LATE = 4
-LAST = 2
+LAST = 3
 EARLY = 0
 TILES = 4
-PRE = (1, 2)
+FLOWS = (1,3,2)
+PRE = (0,1)
 GO = (1, 2, 0)
 BOTH = (((0,), (0,)), ((), ()))
 BACK = (((1,), (1,)), ((), ()))
@@ -451,6 +452,8 @@
             half_copy(which, 0, group).start()
 
     def half_keep(group):
+        if small:
+            return
         for which in range(2):
             for i in range(half_count(0)):
                 owner = half_owner(which, 0, group, i, True)
@@ -467,14 +470,6 @@
                 sum_u[s * fw : (s + 1) * fw, :] = made[:, width:]
         for group in todo[:half]:
             half_first(group)
-
-    def half_rest():
-        for group in todo[: 0 if small else half]:
-            half_keep(group)
-        for group in todo[half:]:
-            half_first(group)
-        for group in todo[0 if small else half : 0 if small else len(todo)]:
-            half_keep(group)
 
     def half_pass(phase, group):
         side, sub = group
@@ -508,17 +503,8 @@
     block_back(nb - 1, *made)
     for b in range(nb - LATE, nb):
         end_start(b, jnp.where(z == 0, 1, n_g - 2))
-    half_rest()
     steps = list(range(nb - begin, nb + HOP * (n_g - 3)))
-    for phase in range(n_bits):
-        for step in steps[phase : phase + 1]:
-            flow_inner(step)
-        for group in half_groups(phase):
-            half_pass(phase, group)
-    for step in steps[n_bits:]:
-        flow_inner(step)
-
-    for b in range(nb):
+    def land(b):
         @pl.when(z > 0)
         def _():
             row_copy(b, z, True).wait_recv()
@@ -543,7 +529,7 @@
                 part[b, z] + from_left[b, z].astype(F32) + from_right[b, z].astype(F32)
             ).astype(BF16)
 
-    def drain(b, carry):
+    def feature_drain(b, carry):
         @pl.when(z > 0)
         def _():
             own_left(b).wait_send()
@@ -557,6 +543,43 @@
             def _():
                 feature_copy(s, b, fwd_sem.at[b, s], z).wait_send()
 
+        return carry
+
+    def early_drain():
+        lax.fori_loop(0, nb, feature_drain, 0)
+        for which in range(2):
+            for phase, group in groups:
+                weight_whole(which, phase, group).wait_send()
+
+    done = [sum(FLOWS[: phase + 1]) for phase in range(n_bits)]
+    for step in steps[: done[0]]:
+        flow_inner(step)
+    for group in todo[:half]:
+        half_keep(group)
+        half_pass(0, group)
+    for group in todo[half:]:
+        half_first(group)
+    for group in todo[half:]:
+        half_keep(group)
+    for group in todo[half:]:
+        half_pass(0, group)
+    for phase in range(1, n_bits):
+        for step in steps[done[phase - 1] : done[phase]]:
+            flow_inner(step)
+        if phase == n_bits - 1:
+            early_drain()
+            for b in range(nb - LATE):
+                land(b)
+        for group in half_groups(phase):
+            half_pass(phase, group)
+    for step in steps[done[-1] :]:
+        flow_inner(step)
+
+    for b in range(nb - LATE, nb):
+        land(b)
+
+    def row_drain(b, carry):
+        for s in range(n_g):
             @pl.when(s > z)
             def _():
                 row_copy(b, s, True).wait_send()
@@ -567,10 +590,8 @@
 
         return carry
 
-    lax.fori_loop(0, nb, drain, 0)
+    lax.fori_loop(0, nb, row_drain, 0)
     for which in range(2):
-        for phase, group in groups:
-            weight_whole(which, phase, group).wait_send()
         for phase in range(n_bits):
             for group in half_groups(phase):
                 half_copy(which, phase, group).wait_send()

time: 61.9 us -> 60.1 us (0.971)
  Pallas kernels: 60.4 us -> 58.7 us
    pallas_call x1, Pallas kernels: 59 us -> 57.2 us  [shards(): pl.pallas_call(functools.partial(kernel, n_dp, n_g, factor), out_shape=tu...]
where the time goes in v6:
time: 60.1 us; the launch traced here: 60 us
  Pallas kernels  58.7 us (98%)
  between operations  1.29 us (2%)
    pallas_call x1, Pallas kernels, shards(): pl.pallas_call(functools.partial(kernel, n_dp, n_g, factor), out_shape=tu...  57.2 us
    pallas_call x1, Pallas kernels, shards(): pl.pallas_call(store, out_shape=(jax.ShapeDtypeStruct((routed_len, width)...  1.48 us

profile of v6, /device:TPU:0, one launch (start us, length us, event | category | flops | bytes accessed | tf_op | source)
XLA Modules:
  0.0 60.0 jit_solution(15948701309585308435)
XLA Ops:
  1.3 57.2 %shard_map.102 = (bf16[512,256]{1,0:T(8,128)(2,1)S(1)}, f32[256,256]{1,0:T(8,128)S(1)}, f32[256,256]{1,0:T(8,128)S(1)}, bf16[1024,512]{1,0:T(8,128)(2,1)S(1)}, bf16[512,512]{1,0:T(8,128)(2,1)S(1)}) custom-call(bf16[1024,512]{1,0:T(8,128)(2,1)} %tokens_in.1, bf16[256,256]{1,0:T(8,128)(2,1)} %gate_w.1, bf16[256,256]{1,0:T(8,128)(2,1)} %up_w.1, ...), custom_call_target="tpu_custom_call" | custom-call | tf_op jit(solution)/shard_map/pallas_call | solution.py:642
  58.5 1.5 %shard_map.103 = (bf16[512,256]{1,0:T(8,128)(2,1)}, bf16[1024,512]{1,0:T(8,128)(2,1)}, f32[256,256]{1,0:T(8,128)}, f32[256,256]{1,0:T(8,128)}) custom-call(bf16[512,256]{1,0:T(8,128)(2,1)S(1)} %get-tuple-element.9.hidden, f32[256,256]{1,0:T(8,128)S(1)} %get-tuple-element.10.gate, f32[256,256]{1,0:T(8,128)S(1)} %get-tuple-element.11.up, ...), custom_call_target="tpu_custom_call" | custom-call | tf_op jit(solution)/shard_map/pallas_call | solution.py:684

commit v7 on v6

--- a/solution.py
+++ b/solution.py
@@ -33,7 +33,7 @@
     gate_w,
     up_w,
     rows_in,
-    count_in,
+    count,
     route_in,
     grad_in,
     hidden,
@@ -44,7 +44,6 @@
     tokens,
     rows,
     route,
-    count,
     grad_hidden,
     coef,
     routed,
@@ -101,7 +100,6 @@
                 (tokens_in, tokens),
                 (rows_in, rows),
                 (route_in, route),
-                (count_in, count),
                 (gate_w, wg.at[pl.ds(p * w_rows, w_rows)]),
                 (up_w, wu.at[pl.ds(p * w_rows, w_rows)]),
                 (grad_in, grad_hidden),
@@ -251,13 +249,12 @@
         pick(b)
         own_block(b)
     copies_in[2].wait()
-    copies_in[3].wait()
     live = lax.broadcasted_iota(jnp.int32, (n_blocks, block_len), 0) < count[0]
     weights = jnp.where(live, route[...], 0.0)
     for b in range(n_blocks):
         turned = jnp.broadcast_to(weights[b : b + 1, :], (block_len, block_len)).T
         coef[b * block_len : (b + 1) * block_len, :] = turned
-    for copy in copies_in[4:]:
+    for copy in copies_in[3:]:
         copy.wait()
 
     groups = [(phase, group) for phase in range(n_bits) for group in range(phase + 1)]
@@ -631,6 +628,7 @@
     dma = pltpu.SemaphoreType.DMA
     vmem = pl.BlockSpec(memory_space=pltpu.VMEM)
     hbm = pl.BlockSpec(memory_space=pltpu.HBM)
+    smem = pl.BlockSpec(memory_space=pltpu.SMEM)
     outs = (
         ((routed_len, width), BF16),
         ((w_rows, width), F32),
@@ -642,13 +640,12 @@
     made = pl.pallas_call(
         functools.partial(kernel, n_dp, n_g, factor),
         out_shape=tuple(pltpu.VMEM(shape, kind) for shape, kind in outs),
-        in_specs=[hbm] * 7,
+        in_specs=[hbm] * 4 + [smem] + [hbm] * 2,
         out_specs=(vmem,) * len(outs),
         scratch_shapes=[
             pltpu.VMEM((n_tok, fw), BF16),
             pltpu.VMEM((n_blocks, block_len), jnp.int32),
             pltpu.VMEM((n_blocks, block_len), F32),
-            pltpu.SMEM((1,), jnp.int32),
             pltpu.VMEM((routed_len, width), BF16),
             pltpu.VMEM((routed_len, block_len), F32),
             pltpu.VMEM((n_g, routed_len, fw), BF16),
@@ -675,7 +672,7 @@
             dma((nb, n_g)),
             dma((2, n_bits, 4)),
             dma((2, n_bits, 4)),
-            dma((7,)),
+            dma((6,)),
         ],
         compiler_params=pltpu.CompilerParams(
             collective_id=0, has_side_effects=True, vmem_limit_bytes=67043328 - kept

time: 60.1 us -> 60.1 us (level)
  no operation moved by 1% of the time
where the time goes in v7:
time: 60.1 us; the launch traced here: 59.9 us
  Pallas kernels  58.7 us (98%)
  between operations  1.29 us (2%)
    pallas_call x1, Pallas kernels, shards(): pl.pallas_call(functools.partial(kernel, n_dp, n_g, factor), out_shape=tu...  57.2 us
    pallas_call x1, Pallas kernels, shards(): pl.pallas_call(store, out_shape=(jax.ShapeDtypeStruct((routed_len, width)...  1.48 us

profile of v7, /device:TPU:0, one launch (start us, length us, event | category | flops | bytes accessed | tf_op | source)
XLA Modules:
  0.0 59.9 jit_solution(1616174715571167067)
XLA Ops:
  1.3 57.2 %shard_map.102 = (bf16[512,256]{1,0:T(8,128)(2,1)S(1)}, f32[256,256]{1,0:T(8,128)S(1)}, f32[256,256]{1,0:T(8,128)S(1)}, bf16[1024,512]{1,0:T(8,128)(2,1)S(1)}, bf16[512,512]{1,0:T(8,128)(2,1)S(1)}) custom-call(bf16[1024,512]{1,0:T(8,128)(2,1)} %tokens_in.1, bf16[256,256]{1,0:T(8,128)(2,1)} %gate_w.1, bf16[256,256]{1,0:T(8,128)(2,1)} %up_w.1, ...), custom_call_target="tpu_custom_call" | custom-call | tf_op jit(solution)/shard_map/pallas_call | solution.py:640
  58.5 1.5 %shard_map.103 = (bf16[512,256]{1,0:T(8,128)(2,1)}, bf16[1024,512]{1,0:T(8,128)(2,1)}, f32[256,256]{1,0:T(8,128)}, f32[256,256]{1,0:T(8,128)}) custom-call(bf16[512,256]{1,0:T(8,128)(2,1)S(1)} %get-tuple-element.9.hidden, f32[256,256]{1,0:T(8,128)S(1)} %get-tuple-element.10.gate, f32[256,256]{1,0:T(8,128)S(1)} %get-tuple-element.11.up, ...), custom_call_target="tpu_custom_call" | custom-call | tf_op jit(solution)/shard_map/pallas_call | solution.py:681
